TPU v7x, 32 devices: a whole 2x2x4 slice. The times are simulated.
32 devices in a mesh: row: 8 (over y, x, core), col: 4 (over z).
Axes of the slice: x: 2, y: 2, z: 4, core: 2. Of those that a mesh axis runs over, the one named last changes fastest.
Arguments:
- start_vector: float32 [131072], P(('row', 'col'))
- energies: float32 [131072], P(('row', 'col')), may hold values from 0.5 to 4
- tile_values: float32 [8, 1024, 4096], P('row', 'col'), may hold values from -0.375 to 0.375
- tile_rows: int32 [8, 1024], P('row', 'col'), may hold values from 0 to 255, as said below
- tile_cols: int32 [8, 1024], P('row', 'col'), may hold values from 0 to 511, as said below
- tile_counts: int32 [8, 4], P('row', 'col'), may hold values from 1 to 256, as said below
Outputs:
- lanczos_vector: float32 [131072], P(('row', 'col'))
- alphas: float32 [2], replicated
- betas: float32 [2], replicated
Inputs may be any that keep to these rules, and one draw needn't show every extreme that they name: `tile_rows`: every slot's global tile row is at least its global tile column; each local tile row is below 4 * 64. `tile_cols`: each local tile column is below 8 * 64. `tile_counts`: at most 256 live slots on a device, reached on some device in every draw.
All inputs are finite; a program needn't handle non-finite values.
Results may differ from a plain program's by a relative error of at most 0.00016.
Values sent between devices are 32-bit elements; how exact they have to be, the bound alone decides.
A program may use at most 128 MiB of HBM per device.

v0:
```python
import functools

import jax
import jax.numpy as jnp
from jax import lax
from jax.experimental import pallas as pl
from jax.experimental.pallas import tpu as pltpu
from jax.sharding import PartitionSpec as P

TILE = 64
STEPS = 2
LANES = 128
CHUNK = 256
UNROLL = True
MESH = pl.DeviceIdType.MESH
F32 = jnp.float32
BF16 = jnp.bfloat16


def split2(x):
    hi = x.astype(BF16)
    return hi, (x - hi.astype(F32)).astype(BF16)


def pick(one_hot, x):
    both = jnp.dot(one_hot, jnp.concatenate(split2(x), axis=1), preferred_element_type=F32)
    return both[:, :LANES] + both[:, LANES:]


def flipped(me, bits, size):
    out, step = me * 0, 1
    while step < size:
        out += ((me // step + bits // step) % 2) * step
        step *= 2
    return out


def peers_of(me, size):
    if size & (size - 1):
        return [lax.rem(me + o, size) for o in range(1, size)]
    return [flipped(me, bits, size) for bits in range(size - 1, 0, -1)]


def kernel(
    n_row, n_col, total,
    s_hbm, e_hbm, t_hbm, tr_hbm, tc_hbm, cnt_hbm,
    out_ref,
    s_ref, e_ref, tr_ref, tc_ref, cnt_ref, t_ref, w_ref, rowbuf, colbuf, dfull, mfull, drecv, mrecv,
    pay, s1buf, s2buf, paya, buf3,
    oc, orr, oct_, ort, ssum, sexp, xc2, xk, accd, accm, mr_ref, mc_ref,
    in_sem, gc_s, gc_r, gr_s, gr_r, rd_s, rd_r, rm_s, rm_r,
    a1_s, a1_r, a2_s, a2_r, a3_s, a3_r,
):
    r = lax.axis_index("row")
    c = lax.axis_index("col")
    pr = s_ref.shape[0]
    slots = t_ref.shape[0]
    flat = t_ref.shape[1]
    chunks = flat // CHUNK

    load_s, load_tr, load_tc, load_cnt, load_e, load_t = loads = [
        pltpu.make_async_copy(src, dst, in_sem.at[i])
        for i, (src, dst) in enumerate([
            (s_hbm, s_ref), (tr_hbm, tr_ref), (tc_hbm, tc_ref),
            (cnt_hbm, cnt_ref), (e_hbm, e_ref), (t_hbm, t_ref),
        ])
    ]
    for d in loads:
        d.start()

    row_peers = peers_of(r, n_row)
    col_peers = peers_of(c, n_col)

    barrier = pltpu.get_barrier_semaphore()
    for p in row_peers:
        pl.semaphore_signal(barrier, inc=1, device_id=(p, c), device_id_type=MESH)
    for p in col_peers:
        pl.semaphore_signal(barrier, inc=1, device_id=(r, p), device_id_type=MESH)
    pl.semaphore_wait(barrier, n_row + n_col - 2)

    def remote(src, dst, ss, rs, dev):
        return pltpu.make_async_remote_copy(
            src_ref=src, dst_ref=dst, send_sem=ss, recv_sem=rs,
            device_id=dev, device_id_type=MESH,
        )

    def slab(p):
        return pl.ds(pl.multiple_of(p * pr, pr), pr)

    sends = []

    def gather(it, src):
        for o, p in enumerate(row_peers):
            d = remote(src, colbuf.at[it, slab(r)], gc_s.at[it, o], gc_r.at[it, r], (p, c))
            d.start()
            sends.append(d)
        for o, p in enumerate(col_peers):
            d = remote(src, rowbuf.at[it, slab(c)], gr_s.at[it, o], gr_r.at[it, c], (r, p))
            d.start()
            sends.append(d)

    def wait_col(it):
        for o, p in enumerate(row_peers):
            remote(colbuf.at[it, slab(p)], colbuf.at[it, slab(p)], gc_s.at[it, o], gc_r.at[it, p], (p, c)).wait_recv()

    def wait_row(it):
        for o, p in enumerate(col_peers):
            remote(rowbuf.at[it, slab(p)], rowbuf.at[it, slab(p)], gr_s.at[it, o], gr_r.at[it, p], (r, p)).wait_recv()

    def scal_one(k):
        for o, p in enumerate(row_peers):
            d = remote(pay.at[k, 0], s1buf.at[k, r], a1_s.at[k, o], a1_r.at[k, r], (p, c))
            d.start()
            sends.append(d)

    def scal_one_get(k):
        parts = [pay[k, 0]]
        for o, p in enumerate(row_peers):
            remote(s1buf.at[k, p], s1buf.at[k, p], a1_s.at[k, o], a1_r.at[k, p], (p, c)).wait_recv()
            parts.append(s1buf[k, p])
        return parts

    def scal_two(k):
        for o, p in enumerate(col_peers):
            d = remote(pay.at[k, 1], s2buf.at[k, c], a2_s.at[k, o], a2_r.at[k, c], (r, p))
            d.start()
            sends.append(d)

    def scal_two_get(k):
        parts = [pay[k, 1]]
        for o, p in enumerate(col_peers):
            remote(s2buf.at[k, p], s2buf.at[k, p], a2_s.at[k, o], a2_r.at[k, p], (r, p)).wait_recv()
            parts.append(s2buf[k, p])
        return parts

    def whole(x):
        return jnp.broadcast_to(jnp.sum(jnp.sum(x, axis=0, keepdims=True), axis=1, keepdims=True), (1, LANES))

    def moments(v, w):
        vw = whole(v * w)
        vv = whole(v * v)
        mean = jnp.where(vv > 0, vw / jnp.where(vv > 0, vv, 1.0), 0.0)
        z = w - mean * v
        return packed(vw, vv, whole(z * z), mean)

    def packed(vw, vv, zz, mean):
        return jnp.concatenate([vw, vv, zz, mean, jnp.zeros((4, LANES), F32)], axis=0)

    def spread_about(parts, center):
        out = jnp.zeros((1, LANES), F32)
        for q in parts:
            gap = center - q[3:4]
            out += q[2:3] + gap * gap * q[1:2]
        return out

    def merge(parts):
        vw = functools.reduce(jnp.add, [q[0:1] for q in parts])
        vv = functools.reduce(jnp.add, [q[1:2] for q in parts])
        mean = jnp.where(vv > 0, vw / jnp.where(vv > 0, vv, 1.0), 0.0)
        return packed(vw, vv, spread_about(parts, mean), mean)

    def alpha_beta(parts):
        vw = functools.reduce(jnp.add, [q[0:1] for q in parts])
        alpha = vw / total
        beta = jnp.sqrt(spread_about(parts, alpha) / total + 1e-06)
        return alpha, beta

    load_s.wait()
    s = s_ref[...]
    gather(0, s_ref)
    colbuf[0, slab(r)] = s
    rowbuf[0, slab(c)] = s
    pay[0, 0] = jnp.broadcast_to(whole(s * s), (8, LANES))
    scal_one(0)

    lane = lax.broadcasted_iota(jnp.int32, (slots, LANES), 1)
    half = lane // TILE
    slot = lax.broadcasted_iota(jnp.int32, (slots, LANES), 0)
    load_cnt.wait()
    load_tr.wait()
    load_tc.wait()
    live = slot < cnt_ref[0, 0]
    a_row = tr_ref[...]
    b_row = tc_ref[...]
    a_col = jnp.transpose(jnp.broadcast_to(a_row, (LANES, slots)))
    b_col = jnp.transpose(jnp.broadcast_to(b_row, (LANES, slots)))

    def as_one(m):
        return jnp.where(m, 1.0, 0.0).astype(F32)

    a_half = as_one((a_col & 1) == half)
    b_half = as_one((b_col & 1) == half)
    alive = as_one(live)
    mr_ref[0] = a_half
    mr_ref[1] = a_half * alive
    mc_ref[0] = b_half
    mc_ref[1] = b_half * alive
    for h in range(orr.shape[1] // LANES):
        orr[:, h * LANES:(h + 1) * LANES] = as_one((a_col >> 1) == lane + h * LANES).astype(BF16)
    for h in range(oc.shape[1] // LANES):
        oc[:, h * LANES:(h + 1) * LANES] = as_one((b_col >> 1) == lane + h * LANES).astype(BF16)
    ort[...] = as_one(jnp.broadcast_to(a_row >> 1, ort.shape) == lax.broadcasted_iota(jnp.int32, ort.shape, 0)).astype(BF16)
    oct_[...] = as_one(jnp.broadcast_to(b_row >> 1, oct_.shape) == lax.broadcasted_iota(jnp.int32, oct_.shape, 0)).astype(BF16)

    k_sum = lax.broadcasted_iota(jnp.int32, (CHUNK, LANES), 0) // TILE
    n_sum = lax.broadcasted_iota(jnp.int32, (CHUNK, LANES), 1) & (TILE - 1)
    k_exp = lax.broadcasted_iota(jnp.int32, (LANES, CHUNK), 0) & (TILE - 1)
    n_exp = lax.broadcasted_iota(jnp.int32, (LANES, CHUNK), 1) // TILE
    per = CHUNK // TILE

    def build(i, carry):
        rows = pl.ds(pl.multiple_of(i * CHUNK, CHUNK), CHUNK)
        ssum[rows, :] = as_one(n_sum == k_sum + i * per).astype(BF16)
        sexp[:, rows] = as_one(k_exp == n_exp + i * per).astype(BF16)
        return carry

    lax.fori_loop(0, chunks, build, 0)

    def twice(x, mask):
        kept = x * mask
        return kept + pltpu.roll(kept, TILE, 1)

    def direct(it):
        x2 = twice(pick(oc[...], colbuf[it]), mc_ref[0])
        xc2[:, :LANES] = x2
        xc2[:, LANES:] = x2
        accd[...] = jnp.zeros_like(accd)

        def step(i, carry):
            cols = pl.ds(pl.multiple_of(i * CHUNK, CHUNK), CHUNK)
            p = t_ref[:, cols] * xc2[...]
            hi = p.astype(BF16)
            lo = (p - hi.astype(F32)).astype(BF16)
            w = ssum[cols, :]
            accd[...] += jnp.dot(hi, w, preferred_element_type=F32) + jnp.dot(lo, w, preferred_element_type=F32)
            return carry

        lax.fori_loop(0, chunks, step, 0, unroll=UNROLL)
        dfull[it] = pick(ort[...], accd[...] * mr_ref[1])
        for o, p in enumerate(col_peers):
            d = remote(dfull.at[it, slab(p)], drecv.at[it, c], rd_s.at[it, o], rd_r.at[it, c], (r, p))
            d.start()
            sends.append(d)

    def mirror(it):
        x2 = twice(pick(orr[...], rowbuf[it]), mr_ref[0])
        hi = x2.astype(BF16).astype(F32)
        xk[...] = jnp.where(half == 0, hi, x2 - hi).astype(BF16)
        accm[...] = jnp.zeros_like(accm)

        def step(i, carry):
            cols = pl.ds(pl.multiple_of(i * CHUNK, CHUNK), CHUNK)
            p = t_ref[:, cols] * jnp.dot(xk[...], sexp[:, cols], preferred_element_type=F32)
            accm[...] += p[:, :LANES] + p[:, LANES:]
            return carry

        lax.fori_loop(0, chunks, step, 0, unroll=UNROLL)
        m = accm[...]
        mfull[it] = pick(oct_[...], (m + pltpu.roll(m, TILE, 1)) * mc_ref[1])
        for o, p in enumerate(row_peers):
            d = remote(mfull.at[it, slab(p)], mrecv.at[it, r], rm_s.at[it, o], rm_r.at[it, r], (p, c))
            d.start()
            sends.append(d)

    def collect(it, x):
        h = e_ref[...] * x + dfull[it, slab(c)] + mfull[it, slab(r)]
        for o, p in enumerate(col_peers):
            remote(drecv.at[it, p], drecv.at[it, p], rd_s.at[it, o], rd_r.at[it, p], (r, p)).wait_recv()
            h += drecv[it, p]
        for o, p in enumerate(row_peers):
            remote(mrecv.at[it, p], mrecv.at[it, p], rm_s.at[it, o], rm_r.at[it, p], (p, c)).wait_recv()
            h += mrecv[it, p]
        return h

    wait_col(0)
    load_t.wait()
    load_e.wait()
    direct(0)
    parts = scal_one_get(0)
    pay[0, 1] = functools.reduce(jnp.add, parts)
    scal_two(0)
    wait_row(0)
    mirror(0)
    square = functools.reduce(jnp.add, scal_two_get(0))[0:1]
    norm = jnp.sqrt(square / total + 1e-06)
    v0 = s / norm
    w0 = collect(0, s) / norm
    w_ref[...] = w0
    gather(1, w_ref)
    colbuf[1, slab(r)] = w0
    rowbuf[1, slab(c)] = w0
    pay[1, 0] = moments(v0, w0)
    scal_one(1)
    wait_col(1)
    direct(1)
    pay[1, 1] = merge(scal_one_get(1))
    scal_two(1)
    wait_row(1)
    mirror(1)
    alpha0, beta0 = alpha_beta(scal_two_get(1))
    v1 = (w0 - alpha0 * v0) / beta0
    w1 = (collect(1, w0) - alpha0 * w0) / beta0 - beta0 * v0
    mine = moments(v1, w1)
    for i in range(4):
        paya[i] = mine[i:i + 1]
    me = r * n_col + c
    count = n_row * n_col
    others = [lax.rem(me + o, count) for o in range(1, count)]
    last = []
    for o, p in enumerate(others):
        d = remote(paya, buf3.at[me], a3_s.at[o], a3_r.at[me], (p // n_col, lax.rem(p, n_col)))
        d.start()
        last.append(d)
    for d in sends:
        d.wait_send()
    sends.clear()
    parts = [(mine[0:1], mine[1:2], mine[2:3], mine[3:4])]
    for o, p in enumerate(others):
        remote(buf3.at[p], buf3.at[p], a3_s.at[o], a3_r.at[p], (p // n_col, lax.rem(p, n_col))).wait_recv()
    for p in others:
        parts.append(tuple(buf3[p, i] for i in range(4)))
    alpha1 = functools.reduce(jnp.add, [q[0] for q in parts]) / total
    spread = functools.reduce(jnp.add, [q[2] + (alpha1 - q[3]) * (alpha1 - q[3]) * q[1] for q in parts])
    beta1 = jnp.sqrt(spread / total + 1e-06)
    out_ref[:pr] = (w1 - alpha1 * v1) / beta1
    at = lax.broadcasted_iota(jnp.int32, (1, LANES), 1)
    out_ref[pr:] = jnp.concatenate(
        [jnp.where(at == 0, alpha0, alpha1), jnp.where(at == 0, beta0, beta1), jnp.zeros((6, LANES), F32)], axis=0
    )
    for d in last:
        d.wait_send()


def hand_out(in_ref, vec_ref, al_ref, be_ref):
    pr = vec_ref.shape[0]
    vec_ref[...] = in_ref[:pr]
    al_ref[...] = in_ref[pr, :STEPS]
    be_ref[...] = in_ref[pr + 1, :STEPS]


def local(start_vector, energies, tile_values, tile_rows, tile_cols, tile_counts):
    n_row = lax.axis_size("row")
    n_col = lax.axis_size("col")
    piece = start_vector.shape[0]
    pr = piece // LANES
    slots, flat = tile_values.shape[1:]
    rr, cr = n_col * pr, n_row * pr
    vm = pl.BlockSpec(memory_space=pltpu.VMEM)
    dma = pltpu.SemaphoreType.DMA
    out = pl.pallas_call(
        functools.partial(kernel, n_row, n_col, float(piece * n_row * n_col)),
        out_shape=jax.ShapeDtypeStruct((pr + 8, LANES), F32),
        in_specs=[pl.BlockSpec(memory_space=pltpu.HBM)] * 6,
        out_specs=vm,
        scratch_shapes=[
            pltpu.VMEM((pr, LANES), F32),
            pltpu.VMEM((pr, LANES), F32),
            pltpu.VMEM(tile_rows.shape, jnp.int32),
            pltpu.VMEM(tile_cols.shape, jnp.int32),
            pltpu.SMEM(tile_counts.shape, jnp.int32),
            pltpu.VMEM((slots, flat), F32),
            pltpu.VMEM((pr, LANES), F32),
            pltpu.VMEM((2, rr, LANES), F32),
            pltpu.VMEM((2, cr, LANES), F32),
            pltpu.VMEM((2, rr, LANES), F32),
            pltpu.VMEM((2, cr, LANES), F32),
            pltpu.VMEM((2, n_col, pr, LANES), F32),
            pltpu.VMEM((2, n_row, pr, LANES), F32),
            pltpu.VMEM((2, 2, 8, LANES), F32),
            pltpu.VMEM((2, n_row, 8, LANES), F32),
            pltpu.VMEM((2, n_col, 8, LANES), F32),
            pltpu.VMEM((4, 1, LANES), F32),
            pltpu.VMEM((n_row * n_col, 4, 1, LANES), F32),
            pltpu.VMEM((slots, cr), BF16),
            pltpu.VMEM((slots, rr), BF16),
            pltpu.VMEM((cr, slots), BF16),
            pltpu.VMEM((rr, slots), BF16),
            pltpu.VMEM((flat, LANES), BF16),
            pltpu.VMEM((LANES, flat), BF16),
            pltpu.VMEM((slots, CHUNK), F32),
            pltpu.VMEM((slots, LANES), BF16),
            pltpu.VMEM((slots, LANES), F32),
            pltpu.VMEM((slots, LANES), F32),
            pltpu.VMEM((2, slots, LANES), F32),
            pltpu.VMEM((2, slots, LANES), F32),
            dma((6,)),
            dma((2, n_row)), dma((2, n_row)),
            dma((2, n_col)), dma((2, n_col)),
            dma((2, n_col)), dma((2, n_col)),
            dma((2, n_row)), dma((2, n_row)),
            dma((2, n_row)), dma((2, n_row)),
            dma((2, n_col)), dma((2, n_col)),
            dma((n_row * n_col,)), dma((n_row * n_col,)),
        ],
        compiler_params=pltpu.CompilerParams(
            collective_id=0, has_side_effects=True, vmem_limit_bytes=67043328
        ),
    )(
        start_vector.reshape(pr, LANES),
        energies.reshape(pr, LANES),
        tile_values.reshape(slots, flat),
        tile_rows,
        tile_cols,
        tile_counts,
    )
    vector, alphas, betas = pl.pallas_call(
        hand_out,
        out_shape=(
            jax.ShapeDtypeStruct((pr, LANES), F32),
            jax.ShapeDtypeStruct((STEPS,), F32),
            jax.ShapeDtypeStruct((STEPS,), F32),
        ),
        in_specs=[vm],
        out_specs=(vm, vm, vm),
    )(out)
    return vector.reshape(piece), alphas, betas


def solution(mesh):
    placed = (
        P(("row", "col")),
        P(("row", "col")),
        P("row", "col", None),
        P("row", "col"),
        P("row", "col"),
        P("row", "col"),
    )
    return jax.shard_map(
        local, mesh=mesh, in_specs=placed, out_specs=(P(("row", "col")), P(), P()), check_vma=False
    )
```

profile of v0, /device:TPU:0, one launch (start us, length us, event | category | flops | bytes accessed | tf_op | source)
XLA Modules:
  0.0 35.1 jit_solution(3603855934092817043)
XLA Ops:
  1.3 32.5 %shard_map.85.in_ref = f32[40,128]{1,0:T(8,128)} custom-call(f32[32,128]{1,0:T(8,128)} %bitcast.5, f32[32,128]{1,0:T(8,128)} %bitcast.6, f32[256,4096]{1,0:T(8,128)} %bitcast.4, s32[1,256]{1,0:T(1,128)} %tr_hbm.1, s32[1,256]{1,0:T(1,128)} %tc_hbm.1, s32[1,1]{1,0:T(1,128)S(6)} %copy.9.cnt_hbm), custom_call_target="tpu_custom_call" | custom-call | tf_op jit(solution)/shard_map/pallas_call | solution.py:350
  33.8 1.3 %shard_map.86 = (f32[32,128]{1,0:T(8,128)}, f32[2]{0:T(128)}, f32[2]{0:T(128)}) custom-call(f32[40,128]{1,0:T(8,128)} %shard_map.85.in_ref), custom_call_target="tpu_custom_call" | custom-call | tf_op jit(solution)/shard_map/pallas_call | solution.py:406
where the time goes:
time: 35.3 us; the launch traced here: 35.1 us
  Pallas kernels  33.8 us (96%)
  between operations  1.29 us (4%)
    pallas_call x1, Pallas kernels, local(): pl.pallas_call(functools.partial(kernel, n_row, n_col, float(piece * n_ro...  32.5 us
    pallas_call x1, Pallas kernels, local(): pl.pallas_call(hand_out, out_shape=(jax.ShapeDtypeStruct((pr, LANES), F32...  1.34 us

commit v1 on v0

--- a/solution.py
+++ b/solution.py
@@ -349,7 +349,7 @@
     dma = pltpu.SemaphoreType.DMA
     out = pl.pallas_call(
         functools.partial(kernel, n_row, n_col, float(piece * n_row * n_col)),
-        out_shape=jax.ShapeDtypeStruct((pr + 8, LANES), F32),
+        out_shape=pltpu.VMEM((pr + 8, LANES), F32),
         in_specs=[pl.BlockSpec(memory_space=pltpu.HBM)] * 6,
         out_specs=vm,
         scratch_shapes=[
@@ -393,7 +393,7 @@
             dma((n_row * n_col,)), dma((n_row * n_col,)),
         ],
         compiler_params=pltpu.CompilerParams(
-            collective_id=0, has_side_effects=True, vmem_limit_bytes=67043328
+            collective_id=0, has_side_effects=True, vmem_limit_bytes=60000000
         ),
     )(
         start_vector.reshape(pr, LANES),
@@ -412,6 +412,7 @@
         ),
         in_specs=[vm],
         out_specs=(vm, vm, vm),
+        compiler_params=pltpu.CompilerParams(vmem_limit_bytes=1048576),
     )(out)
     return vector.reshape(piece), alphas, betas
 

time: 35.3 us -> 33.9 us (0.960)
  Pallas kernels: 33.8 us -> 32.5 us
    pallas_call x1, Pallas kernels: 1.34 us -> 0.61 us  [local(): pl.pallas_call(hand_out, out_shape=(jax.ShapeDtypeStruct((pr, LANES), F32...]
    pallas_call x1, Pallas kernels: 32.5 us -> 31.9 us  [local(): pl.pallas_call(functools.partial(kernel, n_row, n_col, float(piece * n_ro...]
where the time goes in v1:
time: 33.9 us; the launch traced here: 33.8 us
  Pallas kernels  32.5 us (96%)
  between operations  1.29 us (4%)
    pallas_call x1, Pallas kernels, local(): pl.pallas_call(functools.partial(kernel, n_row, n_col, float(piece * n_ro...  31.9 us

profile of v1, /device:TPU:0, one launch (start us, length us, event | category | flops | bytes accessed | tf_op | source)
XLA Modules:
  0.0 33.8 jit_solution(16909129521624694776)
XLA Ops:
  1.3 31.9 %shard_map.85.in_ref = f32[40,128]{1,0:T(8,128)S(1)} custom-call(f32[32,128]{1,0:T(8,128)} %bitcast.5, f32[32,128]{1,0:T(8,128)} %bitcast.6, f32[256,4096]{1,0:T(8,128)} %bitcast.4, s32[1,256]{1,0:T(1,128)} %tr_hbm.1, s32[1,256]{1,0:T(1,128)} %tc_hbm.1, s32[1,1]{1,0:T(1,128)S(6)} %copy.9.cnt_hbm), custom_call_target="tpu_custom_call" | custom-call | tf_op jit(solution)/shard_map/pallas_call | solution.py:350
  33.2 0.6 %shard_map.86 = (f32[32,128]{1,0:T(8,128)}, f32[2]{0:T(128)}, f32[2]{0:T(128)}) custom-call(f32[40,128]{1,0:T(8,128)S(1)} %shard_map.85.in_ref), custom_call_target="tpu_custom_call" | custom-call | tf_op jit(solution)/shard_map/pallas_call | solution.py:406

commit v2 on v1

--- a/solution.py
+++ b/solution.py
@@ -10,8 +10,8 @@
 TILE = 64
 STEPS = 2
 LANES = 128
-CHUNK = 256
-UNROLL = True
+LOADS = 4
+SUBLANES = 8
 MESH = pl.DeviceIdType.MESH
 F32 = jnp.float32
 BF16 = jnp.bfloat16
@@ -47,7 +47,7 @@
     out_ref,
     s_ref, e_ref, tr_ref, tc_ref, cnt_ref, t_ref, w_ref, rowbuf, colbuf, dfull, mfull, drecv, mrecv,
     pay, s1buf, s2buf, paya, buf3,
-    oc, orr, oct_, ort, ssum, sexp, xc2, xk, accd, accm, mr_ref, mc_ref,
+    oc, orr, oct_, ort, tt, xb, xa, dt,
     in_sem, gc_s, gc_r, gr_s, gr_r, rd_s, rd_r, rm_s, rm_r,
     a1_s, a1_r, a2_s, a2_r, a3_s, a3_r,
 ):
@@ -56,16 +56,20 @@
     pr = s_ref.shape[0]
     slots = t_ref.shape[0]
     flat = t_ref.shape[1]
-    chunks = flat // CHUNK
-
-    load_s, load_tr, load_tc, load_cnt, load_e, load_t = loads = [
+    part = flat // LOADS
+
+    load_s, load_tr, load_tc, load_cnt, load_e = loads = [
         pltpu.make_async_copy(src, dst, in_sem.at[i])
         for i, (src, dst) in enumerate([
             (s_hbm, s_ref), (tr_hbm, tr_ref), (tc_hbm, tc_ref),
-            (cnt_hbm, cnt_ref), (e_hbm, e_ref), (t_hbm, t_ref),
+            (cnt_hbm, cnt_ref), (e_hbm, e_ref),
         ])
     ]
-    for d in loads:
+    load_t = []
+    for i in range(LOADS):
+        cols = pl.ds(i * part, part)
+        load_t.append(pltpu.make_async_copy(t_hbm.at[:, cols], t_ref.at[:, cols], in_sem.at[len(loads) + i]))
+    for d in loads + load_t:
         d.start()
 
     row_peers = peers_of(r, n_row)
@@ -174,12 +178,10 @@
     scal_one(0)
 
     lane = lax.broadcasted_iota(jnp.int32, (slots, LANES), 1)
-    half = lane // TILE
-    slot = lax.broadcasted_iota(jnp.int32, (slots, LANES), 0)
     load_cnt.wait()
     load_tr.wait()
     load_tc.wait()
-    live = slot < cnt_ref[0, 0]
+    live = lax.broadcasted_iota(jnp.int32, (TILE, slots), 1) < cnt_ref[0, 0]
     a_row = tr_ref[...]
     b_row = tc_ref[...]
     a_col = jnp.transpose(jnp.broadcast_to(a_row, (LANES, slots)))
@@ -188,13 +190,6 @@
     def as_one(m):
         return jnp.where(m, 1.0, 0.0).astype(F32)
 
-    a_half = as_one((a_col & 1) == half)
-    b_half = as_one((b_col & 1) == half)
-    alive = as_one(live)
-    mr_ref[0] = a_half
-    mr_ref[1] = a_half * alive
-    mc_ref[0] = b_half
-    mc_ref[1] = b_half * alive
     for h in range(orr.shape[1] // LANES):
         orr[:, h * LANES:(h + 1) * LANES] = as_one((a_col >> 1) == lane + h * LANES).astype(BF16)
     for h in range(oc.shape[1] // LANES):
@@ -202,61 +197,65 @@
     ort[...] = as_one(jnp.broadcast_to(a_row >> 1, ort.shape) == lax.broadcasted_iota(jnp.int32, ort.shape, 0)).astype(BF16)
     oct_[...] = as_one(jnp.broadcast_to(b_row >> 1, oct_.shape) == lax.broadcasted_iota(jnp.int32, oct_.shape, 0)).astype(BF16)
 
-    k_sum = lax.broadcasted_iota(jnp.int32, (CHUNK, LANES), 0) // TILE
-    n_sum = lax.broadcasted_iota(jnp.int32, (CHUNK, LANES), 1) & (TILE - 1)
-    k_exp = lax.broadcasted_iota(jnp.int32, (LANES, CHUNK), 0) & (TILE - 1)
-    n_exp = lax.broadcasted_iota(jnp.int32, (LANES, CHUNK), 1) // TILE
-    per = CHUNK // TILE
-
-    def build(i, carry):
-        rows = pl.ds(pl.multiple_of(i * CHUNK, CHUNK), CHUNK)
-        ssum[rows, :] = as_one(n_sum == k_sum + i * per).astype(BF16)
-        sexp[:, rows] = as_one(k_exp == n_exp + i * per).astype(BF16)
-        return carry
-
-    lax.fori_loop(0, chunks, build, 0)
-
-    def twice(x, mask):
-        kept = x * mask
-        return kept + pltpu.roll(kept, TILE, 1)
+    a_odd = jnp.broadcast_to(a_row & 1, (TILE, slots)) == 1
+    b_odd = jnp.broadcast_to(b_row & 1, (TILE, slots)) == 1
+
+    for i in range(flat // LANES):
+        if i * LANES % part == 0:
+            load_t[i * LANES // part].wait()
+        cols = slice(i * LANES, (i + 1) * LANES)
+        tt[cols, :] = jnp.transpose(t_ref[:, cols])
+
+    def gathered(one_hot, x, odd):
+        g = jnp.transpose(pick(one_hot, x))
+        return jnp.where(odd, g[TILE:], g[:TILE])
+
+    def scattered(one_hot, y, odd):
+        zero = jnp.zeros_like(y)
+        even_part = jnp.where(odd, zero, jnp.where(live, y, zero))
+        odd_part = jnp.where(odd, jnp.where(live, y, zero), zero)
+        both = lax.dot_general(
+            one_hot, jnp.concatenate(split2(jnp.concatenate([even_part, odd_part], axis=0)), axis=0),
+            (((1,), (1,)), ((), ())), preferred_element_type=F32,
+        )
+        return both[:, :LANES] + both[:, LANES:]
+
+    sub = lax.broadcasted_iota(jnp.int32, (SUBLANES, slots), 0)
+
+    def fold(parts):
+        shift = 1
+        while len(parts) > 1:
+            low = (sub & shift) == 0
+            parts = [
+                jnp.where(low, p, q) + pltpu.roll(jnp.where(low, q, p), shift, 0)
+                for p, q in zip(parts[::2], parts[1::2])
+            ]
+            shift *= 2
+        return parts[0]
 
     def direct(it):
-        x2 = twice(pick(oc[...], colbuf[it]), mc_ref[0])
-        xc2[:, :LANES] = x2
-        xc2[:, LANES:] = x2
-        accd[...] = jnp.zeros_like(accd)
-
-        def step(i, carry):
-            cols = pl.ds(pl.multiple_of(i * CHUNK, CHUNK), CHUNK)
-            p = t_ref[:, cols] * xc2[...]
-            hi = p.astype(BF16)
-            lo = (p - hi.astype(F32)).astype(BF16)
-            w = ssum[cols, :]
-            accd[...] += jnp.dot(hi, w, preferred_element_type=F32) + jnp.dot(lo, w, preferred_element_type=F32)
-            return carry
-
-        lax.fori_loop(0, chunks, step, 0, unroll=UNROLL)
-        dfull[it] = pick(ort[...], accd[...] * mr_ref[1])
+        xb[...] = gathered(oc[...], colbuf[it], b_odd)
+        for g in range(TILE // SUBLANES):
+            parts = []
+            for a in range(g * SUBLANES, (g + 1) * SUBLANES):
+                terms = [
+                    tt[a * TILE + q:a * TILE + q + SUBLANES, :] * xb[q:q + SUBLANES, :]
+                    for q in range(0, TILE, SUBLANES)
+                ]
+                parts.append(functools.reduce(jnp.add, terms))
+            dt[g * SUBLANES:(g + 1) * SUBLANES, :] = fold(parts)
+        dfull[it] = scattered(ort[...], dt[...], a_odd)
         for o, p in enumerate(col_peers):
             d = remote(dfull.at[it, slab(p)], drecv.at[it, c], rd_s.at[it, o], rd_r.at[it, c], (r, p))
             d.start()
             sends.append(d)
 
     def mirror(it):
-        x2 = twice(pick(orr[...], rowbuf[it]), mr_ref[0])
-        hi = x2.astype(BF16).astype(F32)
-        xk[...] = jnp.where(half == 0, hi, x2 - hi).astype(BF16)
-        accm[...] = jnp.zeros_like(accm)
-
-        def step(i, carry):
-            cols = pl.ds(pl.multiple_of(i * CHUNK, CHUNK), CHUNK)
-            p = t_ref[:, cols] * jnp.dot(xk[...], sexp[:, cols], preferred_element_type=F32)
-            accm[...] += p[:, :LANES] + p[:, LANES:]
-            return carry
-
-        lax.fori_loop(0, chunks, step, 0, unroll=UNROLL)
-        m = accm[...]
-        mfull[it] = pick(oct_[...], (m + pltpu.roll(m, TILE, 1)) * mc_ref[1])
+        xa[...] = gathered(orr[...], rowbuf[it], a_odd)
+        m = jnp.zeros((TILE, slots), F32)
+        for a in range(TILE):
+            m += tt[a * TILE:(a + 1) * TILE, :] * xa[a:a + 1, :]
+        mfull[it] = scattered(oct_[...], m, b_odd)
         for o, p in enumerate(row_peers):
             d = remote(mfull.at[it, slab(p)], mrecv.at[it, r], rm_s.at[it, o], rm_r.at[it, r], (p, c))
             d.start()
@@ -272,9 +271,8 @@
             h += mrecv[it, p]
         return h
 
+    load_e.wait()
     wait_col(0)
-    load_t.wait()
-    load_e.wait()
     direct(0)
     parts = scal_one_get(0)
     pay[0, 1] = functools.reduce(jnp.add, parts)
@@ -375,15 +373,11 @@
             pltpu.VMEM((slots, rr), BF16),
             pltpu.VMEM((cr, slots), BF16),
             pltpu.VMEM((rr, slots), BF16),
-            pltpu.VMEM((flat, LANES), BF16),
-            pltpu.VMEM((LANES, flat), BF16),
-            pltpu.VMEM((slots, CHUNK), F32),
-            pltpu.VMEM((slots, LANES), BF16),
-            pltpu.VMEM((slots, LANES), F32),
-            pltpu.VMEM((slots, LANES), F32),
-            pltpu.VMEM((2, slots, LANES), F32),
-            pltpu.VMEM((2, slots, LANES), F32),
-            dma((6,)),
+            pltpu.VMEM((flat, slots), F32),
+            pltpu.VMEM((TILE, slots), F32),
+            pltpu.VMEM((TILE, slots), F32),
+            pltpu.VMEM((TILE, slots), F32),
+            dma((5 + LOADS,)),
             dma((2, n_row)), dma((2, n_row)),
             dma((2, n_col)), dma((2, n_col)),
             dma((2, n_col)), dma((2, n_col)),

time: 33.9 us -> 31.5 us (0.929)
  Pallas kernels: 32.5 us -> 30.1 us
    pallas_call x1, Pallas kernels: 31.9 us -> 29.4 us  [local(): pl.pallas_call(functools.partial(kernel, n_row, n_col, float(piece * n_ro...]
where the time goes in v2:
time: 31.5 us; the launch traced here: 31.3 us
  Pallas kernels  30.1 us (96%)
  between operations  1.29 us (4%)
    pallas_call x1, Pallas kernels, local(): pl.pallas_call(functools.partial(kernel, n_row, n_col, float(piece * n_ro...  29.4 us

profile of v2, /device:TPU:0, one launch (start us, length us, event | category | flops | bytes accessed | tf_op | source)
XLA Modules:
  0.0 31.3 jit_solution(253375617558882181)
XLA Ops:
  1.3 29.4 %shard_map.85.in_ref = f32[40,128]{1,0:T(8,128)S(1)} custom-call(f32[32,128]{1,0:T(8,128)} %bitcast.5, f32[32,128]{1,0:T(8,128)} %bitcast.6, f32[256,4096]{1,0:T(8,128)} %bitcast.4, s32[1,256]{1,0:T(1,128)} %tr_hbm.1, s32[1,256]{1,0:T(1,128)} %tc_hbm.1, s32[1,1]{1,0:T(1,128)S(6)} %copy.9.cnt_hbm), custom_call_target="tpu_custom_call" | custom-call | tf_op jit(solution)/shard_map/pallas_call | solution.py:348
  30.7 0.6 %shard_map.86 = (f32[32,128]{1,0:T(8,128)}, f32[2]{0:T(128)}, f32[2]{0:T(128)}) custom-call(f32[40,128]{1,0:T(8,128)S(1)} %shard_map.85.in_ref), custom_call_target="tpu_custom_call" | custom-call | tf_op jit(solution)/shard_map/pallas_call | solution.py:400

commit v3 on v2

--- a/solution.py
+++ b/solution.py
@@ -92,50 +92,51 @@
         return pl.ds(pl.multiple_of(p * pr, pr), pr)
 
     sends = []
+    near = (row_peers[0], c)
+
+    def spread_out(copies, span, ss, rs):
+        for src, dst, dev in copies:
+            remote(src, dst, ss, rs, dev).start()
+        sends.append(remote(span, span, ss, rs, near))
+
+    def all_in(span, ss, rs):
+        remote(span, span, ss, rs, near).wait_recv()
+
+    def col_span(it):
+        return colbuf.at[it, pl.ds(0, (n_row - 1) * pr)]
+
+    def row_span(it):
+        return rowbuf.at[it, pl.ds(0, (n_col - 1) * pr)]
 
     def gather(it, src):
-        for o, p in enumerate(row_peers):
-            d = remote(src, colbuf.at[it, slab(r)], gc_s.at[it, o], gc_r.at[it, r], (p, c))
-            d.start()
-            sends.append(d)
-        for o, p in enumerate(col_peers):
-            d = remote(src, rowbuf.at[it, slab(c)], gr_s.at[it, o], gr_r.at[it, c], (r, p))
-            d.start()
-            sends.append(d)
+        spread_out([(src, colbuf.at[it, slab(r)], (p, c)) for p in row_peers], col_span(it), gc_s.at[it], gc_r.at[it])
+        spread_out([(src, rowbuf.at[it, slab(c)], (r, p)) for p in col_peers], row_span(it), gr_s.at[it], gr_r.at[it])
 
     def wait_col(it):
-        for o, p in enumerate(row_peers):
-            remote(colbuf.at[it, slab(p)], colbuf.at[it, slab(p)], gc_s.at[it, o], gc_r.at[it, p], (p, c)).wait_recv()
+        all_in(col_span(it), gc_s.at[it], gc_r.at[it])
 
     def wait_row(it):
-        for o, p in enumerate(col_peers):
-            remote(rowbuf.at[it, slab(p)], rowbuf.at[it, slab(p)], gr_s.at[it, o], gr_r.at[it, p], (r, p)).wait_recv()
+        all_in(row_span(it), gr_s.at[it], gr_r.at[it])
 
     def scal_one(k):
-        for o, p in enumerate(row_peers):
-            d = remote(pay.at[k, 0], s1buf.at[k, r], a1_s.at[k, o], a1_r.at[k, r], (p, c))
-            d.start()
-            sends.append(d)
+        spread_out(
+            [(pay.at[k, 0], s1buf.at[k, r], (p, c)) for p in row_peers],
+            s1buf.at[k, pl.ds(0, n_row - 1)], a1_s.at[k], a1_r.at[k],
+        )
 
     def scal_one_get(k):
-        parts = [pay[k, 0]]
-        for o, p in enumerate(row_peers):
-            remote(s1buf.at[k, p], s1buf.at[k, p], a1_s.at[k, o], a1_r.at[k, p], (p, c)).wait_recv()
-            parts.append(s1buf[k, p])
-        return parts
+        all_in(s1buf.at[k, pl.ds(0, n_row - 1)], a1_s.at[k], a1_r.at[k])
+        return [pay[k, 0]] + [s1buf[k, p] for p in row_peers]
 
     def scal_two(k):
-        for o, p in enumerate(col_peers):
-            d = remote(pay.at[k, 1], s2buf.at[k, c], a2_s.at[k, o], a2_r.at[k, c], (r, p))
-            d.start()
-            sends.append(d)
+        spread_out(
+            [(pay.at[k, 1], s2buf.at[k, c], (r, p)) for p in col_peers],
+            s2buf.at[k, pl.ds(0, n_col - 1)], a2_s.at[k], a2_r.at[k],
+        )
 
     def scal_two_get(k):
-        parts = [pay[k, 1]]
-        for o, p in enumerate(col_peers):
-            remote(s2buf.at[k, p], s2buf.at[k, p], a2_s.at[k, o], a2_r.at[k, p], (r, p)).wait_recv()
-            parts.append(s2buf[k, p])
-        return parts
+        all_in(s2buf.at[k, pl.ds(0, n_col - 1)], a2_s.at[k], a2_r.at[k])
+        return [pay[k, 1]] + [s2buf[k, p] for p in col_peers]
 
     def whole(x):
         return jnp.broadcast_to(jnp.sum(jnp.sum(x, axis=0, keepdims=True), axis=1, keepdims=True), (1, LANES))
@@ -245,10 +246,10 @@
                 parts.append(functools.reduce(jnp.add, terms))
             dt[g * SUBLANES:(g + 1) * SUBLANES, :] = fold(parts)
         dfull[it] = scattered(ort[...], dt[...], a_odd)
-        for o, p in enumerate(col_peers):
-            d = remote(dfull.at[it, slab(p)], drecv.at[it, c], rd_s.at[it, o], rd_r.at[it, c], (r, p))
-            d.start()
-            sends.append(d)
+        spread_out(
+            [(dfull.at[it, slab(p)], drecv.at[it, c], (r, p)) for p in col_peers],
+            drecv.at[it, pl.ds(0, n_col - 1)], rd_s.at[it], rd_r.at[it],
+        )
 
     def mirror(it):
         xa[...] = gathered(orr[...], rowbuf[it], a_odd)
@@ -256,18 +257,18 @@
         for a in range(TILE):
             m += tt[a * TILE:(a + 1) * TILE, :] * xa[a:a + 1, :]
         mfull[it] = scattered(oct_[...], m, b_odd)
-        for o, p in enumerate(row_peers):
-            d = remote(mfull.at[it, slab(p)], mrecv.at[it, r], rm_s.at[it, o], rm_r.at[it, r], (p, c))
-            d.start()
-            sends.append(d)
+        spread_out(
+            [(mfull.at[it, slab(p)], mrecv.at[it, r], (p, c)) for p in row_peers],
+            mrecv.at[it, pl.ds(0, n_row - 1)], rm_s.at[it], rm_r.at[it],
+        )
 
     def collect(it, x):
         h = e_ref[...] * x + dfull[it, slab(c)] + mfull[it, slab(r)]
-        for o, p in enumerate(col_peers):
-            remote(drecv.at[it, p], drecv.at[it, p], rd_s.at[it, o], rd_r.at[it, p], (r, p)).wait_recv()
+        all_in(drecv.at[it, pl.ds(0, n_col - 1)], rd_s.at[it], rd_r.at[it])
+        for p in col_peers:
             h += drecv[it, p]
-        for o, p in enumerate(row_peers):
-            remote(mrecv.at[it, p], mrecv.at[it, p], rm_s.at[it, o], rm_r.at[it, p], (p, c)).wait_recv()
+        all_in(mrecv.at[it, pl.ds(0, n_row - 1)], rm_s.at[it], rm_r.at[it])
+        for p in row_peers:
             h += mrecv[it, p]
         return h
 
@@ -298,35 +299,41 @@
     alpha0, beta0 = alpha_beta(scal_two_get(1))
     v1 = (w0 - alpha0 * v0) / beta0
     w1 = (collect(1, w0) - alpha0 * w0) / beta0 - beta0 * v0
+    at = lax.broadcasted_iota(jnp.int32, (1, LANES), 1)
+    quarter = at // (LANES // 4)
+
+    def part(x, q):
+        return jnp.where(quarter == q, x, 0.0)
+
+    def share(x):
+        x = x + pltpu.roll(x, LANES // 4, 1)
+        return x + pltpu.roll(x, LANES // 2, 1)
+
     mine = moments(v1, w1)
-    for i in range(4):
-        paya[i] = mine[i:i + 1]
     me = r * n_col + c
     count = n_row * n_col
-    others = [lax.rem(me + o, count) for o in range(1, count)]
-    last = []
-    for o, p in enumerate(others):
-        d = remote(paya, buf3.at[me], a3_s.at[o], a3_r.at[me], (p // n_col, lax.rem(p, n_col)))
-        d.start()
-        last.append(d)
+    row = part(mine[0:1], 0) + part(mine[2:3], 1) + part(mine[1:2], 2) + part(mine[3:4], 3)
+    buf3[me] = row
+    paya[...] = row
+    others = [(p, q) for p in row_peers + [r] for q in col_peers + [c]][:-1]
+    span = buf3.at[pl.ds(0, count - 1)]
+    for p, q in others:
+        remote(paya, buf3.at[me], a3_s, a3_r, (p, q)).start()
     for d in sends:
         d.wait_send()
-    sends.clear()
-    parts = [(mine[0:1], mine[1:2], mine[2:3], mine[3:4])]
-    for o, p in enumerate(others):
-        remote(buf3.at[p], buf3.at[p], a3_s.at[o], a3_r.at[p], (p // n_col, lax.rem(p, n_col))).wait_recv()
-    for p in others:
-        parts.append(tuple(buf3[p, i] for i in range(4)))
-    alpha1 = functools.reduce(jnp.add, [q[0] for q in parts]) / total
-    spread = functools.reduce(jnp.add, [q[2] + (alpha1 - q[3]) * (alpha1 - q[3]) * q[1] for q in parts])
-    beta1 = jnp.sqrt(spread / total + 1e-06)
+    all_in(span, a3_s, a3_r)
+    rows = [buf3[i] for i in range(count)]
+    total_row = functools.reduce(jnp.add, rows)
+    alpha1 = share(part(total_row, 0)) / total
+    gaps = functools.reduce(
+        jnp.add, [(alpha1 - q) * (alpha1 - q) * pltpu.roll(q, LANES // 4, 1) for q in rows]
+    )
+    beta1 = jnp.sqrt(share(part(gaps, 3) + part(total_row, 1)) / total + 1e-06)
     out_ref[:pr] = (w1 - alpha1 * v1) / beta1
-    at = lax.broadcasted_iota(jnp.int32, (1, LANES), 1)
     out_ref[pr:] = jnp.concatenate(
         [jnp.where(at == 0, alpha0, alpha1), jnp.where(at == 0, beta0, beta1), jnp.zeros((6, LANES), F32)], axis=0
     )
-    for d in last:
-        d.wait_send()
+    remote(span, span, a3_s, a3_r, near).wait_send()
 
 
 def hand_out(in_ref, vec_ref, al_ref, be_ref):
@@ -367,8 +374,8 @@
             pltpu.VMEM((2, 2, 8, LANES), F32),
             pltpu.VMEM((2, n_row, 8, LANES), F32),
             pltpu.VMEM((2, n_col, 8, LANES), F32),
-            pltpu.VMEM((4, 1, LANES), F32),
-            pltpu.VMEM((n_row * n_col, 4, 1, LANES), F32),
+            pltpu.VMEM((1, LANES), F32),
+            pltpu.VMEM((n_row * n_col, 1, LANES), F32),
             pltpu.VMEM((slots, cr), BF16),
             pltpu.VMEM((slots, rr), BF16),
             pltpu.VMEM((cr, slots), BF16),
@@ -378,13 +385,8 @@
             pltpu.VMEM((TILE, slots), F32),
             pltpu.VMEM((TILE, slots), F32),
             dma((5 + LOADS,)),
-            dma((2, n_row)), dma((2, n_row)),
-            dma((2, n_col)), dma((2, n_col)),
-            dma((2, n_col)), dma((2, n_col)),
-            dma((2, n_row)), dma((2, n_row)),
-            dma((2, n_row)), dma((2, n_row)),
-            dma((2, n_col)), dma((2, n_col)),
-            dma((n_row * n_col,)), dma((n_row * n_col,)),
+            *[dma((2,))] * 12,
+            dma(()), dma(()),
         ],
         compiler_params=pltpu.CompilerParams(
             collective_id=0, has_side_effects=True, vmem_limit_bytes=60000000

time: 31.5 us -> 30 us (0.952)
  Pallas kernels: 30.1 us -> 28.5 us
    pallas_call x1, Pallas kernels: 29.4 us -> 27.9 us  [local(): pl.pallas_call(functools.partial(kernel, n_row, n_col, float(piece * n_ro...]
where the time goes in v3:
time: 30 us; the launch traced here: 29.8 us
  Pallas kernels  28.5 us (95%)
  between operations  1.29 us (4%)
    pallas_call x1, Pallas kernels, local(): pl.pallas_call(functools.partial(kernel, n_row, n_col, float(piece * n_ro...  27.9 us
    pallas_call x1, Pallas kernels, local(): pl.pallas_call(hand_out, out_shape=(jax.ShapeDtypeStruct((pr, LANES), F32...  0.61 us

profile of v3, /device:TPU:0, one launch (start us, length us, event | category | flops | bytes accessed | tf_op | source)
XLA Modules:
  0.0 29.8 jit_solution(4933595052079750908)
XLA Ops:
  1.3 27.9 %shard_map.85.in_ref = f32[40,128]{1,0:T(8,128)S(1)} custom-call(f32[32,128]{1,0:T(8,128)} %bitcast.5, f32[32,128]{1,0:T(8,128)} %bitcast.6, f32[256,4096]{1,0:T(8,128)} %bitcast.4, s32[1,256]{1,0:T(1,128)} %tr_hbm.1, s32[1,256]{1,0:T(1,128)} %tc_hbm.1, s32[1,1]{1,0:T(1,128)S(6)} %copy.9.cnt_hbm), custom_call_target="tpu_custom_call" | custom-call | tf_op jit(solution)/shard_map/pallas_call | solution.py:355
  29.2 0.6 %shard_map.86 = (f32[32,128]{1,0:T(8,128)}, f32[2]{0:T(128)}, f32[2]{0:T(128)}) custom-call(f32[40,128]{1,0:T(8,128)S(1)} %shard_map.85.in_ref), custom_call_target="tpu_custom_call" | custom-call | tf_op jit(solution)/shard_map/pallas_call | solution.py:402

commit v4 on v3

--- a/solution.py
+++ b/solution.py
@@ -49,7 +49,7 @@
     pay, s1buf, s2buf, paya, buf3,
     oc, orr, oct_, ort, tt, xb, xa, dt,
     in_sem, gc_s, gc_r, gr_s, gr_r, rd_s, rd_r, rm_s, rm_r,
-    a1_s, a1_r, a2_s, a2_r, a3_s, a3_r,
+    a1_s, a1_r, a2_s, a2_r, a3_s, a3_r, g0_s, g0_r,
 ):
     r = lax.axis_index("row")
     c = lax.axis_index("col")
@@ -78,9 +78,17 @@
     barrier = pltpu.get_barrier_semaphore()
     for p in row_peers:
         pl.semaphore_signal(barrier, inc=1, device_id=(p, c), device_id_type=MESH)
-    for p in col_peers:
+    above = [(o, c + o, c + o < n_col) for o in range(1, n_col)]
+    below = [(o, c - o, c >= o) for o in range(1, n_col)]
+    has_next = c + 1 < n_col
+
+    def greet(p):
         pl.semaphore_signal(barrier, inc=1, device_id=(r, p), device_id_type=MESH)
-    pl.semaphore_wait(barrier, n_row + n_col - 2)
+
+    for o, p, there in above:
+        pl.when(there)(functools.partial(greet, p))
+    pl.when(c >= 1)(functools.partial(greet, c - 1))
+    pl.semaphore_wait(barrier, n_row - 1 + c + lax.rem(jnp.minimum(c + 1, n_col - 1) + n_col - c, n_col))
 
     def remote(src, dst, ss, rs, dev):
         return pltpu.make_async_remote_copy(
@@ -108,8 +116,38 @@
     def row_span(it):
         return rowbuf.at[it, pl.ds(0, (n_col - 1) * pr)]
 
+    def piece(k, ss, p):
+        return remote(rowbuf.at[0, slab(k)], rowbuf.at[0, slab(k)], ss, g0_r.at[k], (r, p))
+
+    def own(ss, p):
+        return remote(s_ref, rowbuf.at[0, slab(c)], ss, g0_r.at[c], (r, p))
+
+    def first_gather():
+        gather_col(0, s_ref)
+        for o, p, there in reversed(below):
+            pl.when(there)(lambda o=o, p=p: own(g0_s.at[o], p).start())
+        pl.when(has_next)(lambda: own(g0_s.at[0], c + 1).start())
+
+    def pass_on():
+        for o, k, there in below:
+            pl.when(there)(lambda k=k: piece(k, g0_s.at[0], k).wait_recv())
+            pl.when(jnp.logical_and(there, has_next))(lambda o=o, k=k: piece(k, g0_s.at[n_col + o], c + 1).start())
+
+    def first_row():
+        for o, k, there in above:
+            pl.when(there)(lambda k=k: piece(k, g0_s.at[0], k).wait_recv())
+
+    def first_sent():
+        for o, k, there in below:
+            pl.when(there)(lambda o=o, k=k: own(g0_s.at[o], k).wait_send())
+            pl.when(jnp.logical_and(there, has_next))(lambda o=o, k=k: piece(k, g0_s.at[n_col + o], c + 1).wait_send())
+        pl.when(has_next)(lambda: own(g0_s.at[0], c + 1).wait_send())
+
+    def gather_col(it, src):
+        spread_out([(src, colbuf.at[it, slab(r)], (p, c)) for p in row_peers], col_span(it), gc_s.at[it], gc_r.at[it])
+
     def gather(it, src):
-        spread_out([(src, colbuf.at[it, slab(r)], (p, c)) for p in row_peers], col_span(it), gc_s.at[it], gc_r.at[it])
+        gather_col(it, src)
         spread_out([(src, rowbuf.at[it, slab(c)], (r, p)) for p in col_peers], row_span(it), gr_s.at[it], gr_r.at[it])
 
     def wait_col(it):
@@ -172,7 +210,7 @@
 
     load_s.wait()
     s = s_ref[...]
-    gather(0, s_ref)
+    first_gather()
     colbuf[0, slab(r)] = s
     rowbuf[0, slab(c)] = s
     pay[0, 0] = jnp.broadcast_to(whole(s * s), (8, LANES))
@@ -246,6 +284,8 @@
                 parts.append(functools.reduce(jnp.add, terms))
             dt[g * SUBLANES:(g + 1) * SUBLANES, :] = fold(parts)
         dfull[it] = scattered(ort[...], dt[...], a_odd)
+        if it == 0:
+            first_row()
         spread_out(
             [(dfull.at[it, slab(p)], drecv.at[it, c], (r, p)) for p in col_peers],
             drecv.at[it, pl.ds(0, n_col - 1)], rd_s.at[it], rd_r.at[it],
@@ -272,13 +312,13 @@
             h += mrecv[it, p]
         return h
 
+    pass_on()
     load_e.wait()
     wait_col(0)
     direct(0)
     parts = scal_one_get(0)
     pay[0, 1] = functools.reduce(jnp.add, parts)
     scal_two(0)
-    wait_row(0)
     mirror(0)
     square = functools.reduce(jnp.add, scal_two_get(0))[0:1]
     norm = jnp.sqrt(square / total + 1e-06)
@@ -319,6 +359,7 @@
     span = buf3.at[pl.ds(0, count - 1)]
     for p, q in others:
         remote(paya, buf3.at[me], a3_s, a3_r, (p, q)).start()
+    first_sent()
     for d in sends:
         d.wait_send()
     all_in(span, a3_s, a3_r)
@@ -387,6 +428,7 @@
             dma((5 + LOADS,)),
             *[dma((2,))] * 12,
             dma(()), dma(()),
+            dma((2 * n_col,)), dma((n_col,)),
         ],
         compiler_params=pltpu.CompilerParams(
             collective_id=0, has_side_effects=True, vmem_limit_bytes=60000000

time: 30 us -> 33.7 us (1.12)
  Pallas kernels: 28.5 us -> 32.2 us
    pallas_call x1, Pallas kernels: 27.9 us -> 31.6 us  [local(): pl.pallas_call(functools.partial(kernel, n_row, n_col, float(piece * n_ro...]
where the time goes in v4:
time: 33.7 us; the launch traced here: 33.5 us
  Pallas kernels  32.2 us (96%)
  between operations  1.29 us (4%)
    pallas_call x1, Pallas kernels, local(): pl.pallas_call(functools.partial(kernel, n_row, n_col, float(piece * n_ro...  31.6 us

profile of v4, /device:TPU:0, one launch (start us, length us, event | category | flops | bytes accessed | tf_op | source)
XLA Modules:
  0.0 33.5 jit_solution(13294228686218322495)
XLA Ops:
  1.3 31.6 %shard_map.85.in_ref = f32[40,128]{1,0:T(8,128)S(1)} custom-call(f32[32,128]{1,0:T(8,128)} %bitcast.5, f32[32,128]{1,0:T(8,128)} %bitcast.6, f32[256,4096]{1,0:T(8,128)} %bitcast.4, s32[1,256]{1,0:T(1,128)} %tr_hbm.1, s32[1,256]{1,0:T(1,128)} %tc_hbm.1, s32[1,1]{1,0:T(1,128)S(6)} %copy.9.cnt_hbm), custom_call_target="tpu_custom_call" | custom-call | tf_op jit(solution)/shard_map/pallas_call | solution.py:396
  32.9 0.6 %shard_map.86 = (f32[32,128]{1,0:T(8,128)}, f32[2]{0:T(128)}, f32[2]{0:T(128)}) custom-call(f32[40,128]{1,0:T(8,128)S(1)} %shard_map.85.in_ref), custom_call_target="tpu_custom_call" | custom-call | tf_op jit(solution)/shard_map/pallas_call | solution.py:444

commit v5 on v3

--- a/solution.py
+++ b/solution.py
@@ -245,14 +245,20 @@
                 ]
                 parts.append(functools.reduce(jnp.add, terms))
             dt[g * SUBLANES:(g + 1) * SUBLANES, :] = fold(parts)
+
+    def place_direct(it):
         dfull[it] = scattered(ort[...], dt[...], a_odd)
+
+    def send_direct(it):
         spread_out(
             [(dfull.at[it, slab(p)], drecv.at[it, c], (r, p)) for p in col_peers],
             drecv.at[it, pl.ds(0, n_col - 1)], rd_s.at[it], rd_r.at[it],
         )
 
+    def pick_row(it):
+        xa[...] = gathered(orr[...], rowbuf[it], a_odd)
+
     def mirror(it):
-        xa[...] = gathered(orr[...], rowbuf[it], a_odd)
         m = jnp.zeros((TILE, slots), F32)
         for a in range(TILE):
             m += tt[a * TILE:(a + 1) * TILE, :] * xa[a:a + 1, :]
@@ -275,10 +281,13 @@
     load_e.wait()
     wait_col(0)
     direct(0)
+    place_direct(0)
+    send_direct(0)
     parts = scal_one_get(0)
     pay[0, 1] = functools.reduce(jnp.add, parts)
     scal_two(0)
     wait_row(0)
+    pick_row(0)
     mirror(0)
     square = functools.reduce(jnp.add, scal_two_get(0))[0:1]
     norm = jnp.sqrt(square / total + 1e-06)
@@ -292,10 +301,14 @@
     scal_one(1)
     wait_col(1)
     direct(1)
-    pay[1, 1] = merge(scal_one_get(1))
+    wait_row(1)
+    parts = scal_one_get(1)
+    place_direct(1)
+    pick_row(1)
+    pay[1, 1] = merge(parts)
+    send_direct(1)
+    mirror(1)
     scal_two(1)
-    wait_row(1)
-    mirror(1)
     alpha0, beta0 = alpha_beta(scal_two_get(1))
     v1 = (w0 - alpha0 * v0) / beta0
     w1 = (collect(1, w0) - alpha0 * w0) / beta0 - beta0 * v0

time: 30 us -> 30.3 us (1.010)
  Pallas kernels: 28.5 us -> 28.9 us
    pallas_call x1, Pallas kernels: 27.9 us -> 28.3 us  [local(): pl.pallas_call(functools.partial(kernel, n_row, n_col, float(piece * n_ro...]
where the time goes in v5:
time: 30.3 us; the launch traced here: 30.2 us
  Pallas kernels  28.9 us (95%)
  between operations  1.29 us (4%)
    pallas_call x1, Pallas kernels, local(): pl.pallas_call(functools.partial(kernel, n_row, n_col, float(piece * n_ro...  28.3 us
    pallas_call x1, Pallas kernels, local(): pl.pallas_call(hand_out, out_shape=(jax.ShapeDtypeStruct((pr, LANES), F32...  0.61 us

profile of v5, /device:TPU:0, one launch (start us, length us, event | category | flops | bytes accessed | tf_op | source)
XLA Modules:
  0.0 30.2 jit_solution(16225260640796606972)
XLA Ops:
  1.3 28.3 %shard_map.85.in_ref = f32[40,128]{1,0:T(8,128)S(1)} custom-call(f32[32,128]{1,0:T(8,128)} %bitcast.5, f32[32,128]{1,0:T(8,128)} %bitcast.6, f32[256,4096]{1,0:T(8,128)} %bitcast.4, s32[1,256]{1,0:T(1,128)} %tr_hbm.1, s32[1,256]{1,0:T(1,128)} %tc_hbm.1, s32[1,1]{1,0:T(1,128)S(6)} %copy.9.cnt_hbm), custom_call_target="tpu_custom_call" | custom-call | tf_op jit(solution)/shard_map/pallas_call | solution.py:368
  29.6 0.6 %shard_map.86 = (f32[32,128]{1,0:T(8,128)}, f32[2]{0:T(128)}, f32[2]{0:T(128)}) custom-call(f32[40,128]{1,0:T(8,128)S(1)} %shard_map.85.in_ref), custom_call_target="tpu_custom_call" | custom-call | tf_op jit(solution)/shard_map/pallas_call | solution.py:415
